TPU v7x, 128 devices: a whole 4x4x4 slice. The times are simulated.
128 devices in a mesh: grp: 4 (over y), seq: 32 (over z, x, core).
Axes of the slice: x: 4, y: 4, z: 4, core: 2. Of those that a mesh axis runs over, the one named last changes fastest.
Arguments:
- hidden_in: bfloat16 [114688, 1024], P(('grp', 'seq')), may hold values from -16 to 16
- attn_gain: float32 [1024], replicated, may hold values from 0.1 to 1.9
- w_qkv: bfloat16 [1024, 3072], replicated
- head_gain: float32 [1024], replicated, may hold values from 0.1 to 1.9
- w_out: bfloat16 [1024, 1024], replicated, may hold values from -0.1875 to 0.1875
- ffn_gain: float32 [1024], replicated, may hold values from 0.1 to 1.9
- w_gate: bfloat16 [32, 1024, 896], P('seq'), may hold values from -0.1875 to 0.1875
- w_up: bfloat16 [32, 1024, 896], P('seq'), may hold values from -0.1875 to 0.1875
- w_down: bfloat16 [32, 896, 1024], P('seq'), may hold values from -0.1875 to 0.1875
- pair_ids: int32 [896, 2], P(('grp', 'seq')), may hold values from 0 to 31, as said below
- gate_codes: int32 [896, 2], P(('grp', 'seq')), may hold values from 1 to 255
Outputs:
- layer_out: bfloat16 [114688, 1024], P(('grp', 'seq'))
Inputs may be any that keep to these rules, and one draw needn't show every extreme that they name: `pair_ids`: each row names two different experts. Within the 7 rows of one device (aligned blocks of 7 rows) no expert is named more than 2 times, and some expert exactly 2 times. Within the rows of one group (aligned blocks of 224 rows) exactly one expert is named 28 times, every other at most 14 times and some other exactly 14 times; the expert named 28 times differs from group to group.
All inputs are finite; a program needn't handle non-finite values.
Results may differ from a plain program's by a relative error of at most 0.0055.
Values may be sent and summed in bfloat16 or wider, within the bound.
A program may use at most 192 MiB of HBM per device.

v0:
```python
import jax
import jax.numpy as jnp
from jax import lax
from jax.sharding import PartitionSpec as P

HEADS = 8
HEAD_DIM = 128
ROWS = 128
SPAN = 128
CAP = 2


EPS = 1e-06
HIGH = lax.Precision.HIGHEST


def carried_in(part, axis, combine, identity):
    place = lax.axis_index(axis)
    gathered = jax.tree.map(lambda a: lax.all_gather(a, axis), part)
    state = jax.tree.map(lambda a, e: jnp.zeros_like(a) + jnp.asarray(e, a.dtype), part, identity)

    def one(lap, state):
        return combine(
            state, jax.tree.map(lambda a: lax.dynamic_index_in_dim(a, lap, 0, False), gathered)
        )

    return lax.fori_loop(0, place, one, state)


def norm_rows(values, gain):
    return values * lax.rsqrt(jnp.mean(values * values, axis=-1, keepdims=True) + EPS) * gain


def add_pair(earlier, later):
    return (earlier[0] + later[0], earlier[1] + later[1])


def expert_rows(rows_in, gate_weight, up_weight, down_weight):
    gate = jnp.dot(rows_in, gate_weight, preferred_element_type=jnp.float32)
    upper = jnp.dot(rows_in, up_weight, preferred_element_type=jnp.float32)
    inner = (jax.nn.silu(gate) * upper).astype(jnp.bfloat16)
    return jnp.dot(inner, down_weight, preferred_element_type=jnp.float32).astype(jnp.bfloat16)


def body(
    hidden_in,
    attn_gain,
    w_qkv,
    head_gain,
    w_out,
    ffn_gain,
    w_gate,
    w_up,
    w_down,
    pair_ids,
    gate_codes,
):
    tokens = hidden_in.shape[0]
    width = hidden_in.shape[1]
    pieces = tokens // SPAN
    routed = tokens // ROWS
    inputs = hidden_in.astype(jnp.float32)
    normed = norm_rows(inputs, attn_gain).astype(jnp.bfloat16)
    mixed = jnp.dot(normed, w_qkv, preferred_element_type=jnp.float32)
    query = (
        (jax.nn.elu(mixed[:, :width]) + 1.0)
        .astype(jnp.bfloat16)
        .reshape(pieces, SPAN, HEADS, HEAD_DIM)
    )
    keys = (
        (jax.nn.elu(mixed[:, width : 2 * width]) + 1.0)
        .astype(jnp.bfloat16)
        .reshape(pieces, SPAN, HEADS, HEAD_DIM)
    )
    values = mixed[:, 2 * width :].astype(jnp.bfloat16).reshape(pieces, SPAN, HEADS, HEAD_DIM)
    block_state = jnp.einsum("nshd,nshe->nhde", keys, values, preferred_element_type=jnp.float32)
    block_keys = jnp.sum(keys.astype(jnp.float32), axis=1)
    local_state = jnp.sum(block_state, axis=0)
    local_keys = jnp.sum(block_keys, axis=0)
    empty = (jnp.zeros_like(local_state), jnp.zeros_like(local_keys))
    prior_state, prior_keys = carried_in((local_state, local_keys), ("grp", "seq"), add_pair, empty)
    before_state = prior_state[None] + jnp.cumsum(block_state, axis=0) - block_state
    before_keys = prior_keys[None] + jnp.cumsum(block_keys, axis=0) - block_keys
    scores = jnp.einsum("nchd,nshd->nhcs", query, keys, preferred_element_type=jnp.float32)
    causal = lax.broadcasted_iota(jnp.int32, (SPAN, SPAN), 0) >= lax.broadcasted_iota(
        jnp.int32, (SPAN, SPAN), 1
    )
    scores = jnp.where(causal[None, None], scores, jnp.float32(0.0))
    query_wide = query.astype(jnp.float32)
    numer = jnp.einsum("nhcs,nshe->nche", scores, values.astype(jnp.float32), precision=HIGH)
    numer = numer + jnp.einsum("nchd,nhde->nche", query_wide, before_state, precision=HIGH)
    denom = jnp.transpose(jnp.sum(scores, axis=-1), (0, 2, 1)) + jnp.einsum(
        "nchd,nhd->nch", query_wide, before_keys, precision=HIGH
    )
    ratio = (numer / denom[..., None]).reshape(tokens, width)
    attended = norm_rows(ratio, head_gain).astype(jnp.bfloat16)
    resid = (inputs + jnp.dot(attended, w_out, preferred_element_type=jnp.float32)).astype(
        jnp.bfloat16
    )
    ffn_in = norm_rows(resid.astype(jnp.float32), ffn_gain).astype(jnp.bfloat16)
    owners_count = lax.axis_size("seq")
    slots = CAP * owners_count
    limit = min(4 * routed, slots)
    visits = 2 * routed
    flat_ids = pair_ids.reshape(visits)
    lower = lax.broadcasted_iota(jnp.int32, (visits, visits), 1) < lax.broadcasted_iota(
        jnp.int32, (visits, visits), 0
    )
    same = flat_ids[:, None] == flat_ids[None, :]
    slot_rank = jnp.sum((same & lower).astype(jnp.int32), axis=1)
    target = flat_ids * CAP + slot_rank
    slot_ids = lax.broadcasted_iota(jnp.int32, (slots, visits), 0)
    hits = slot_ids == target[None, :]
    chooser = jnp.any(hits.reshape(slots, routed, 2), axis=2).astype(jnp.bfloat16)
    outgoing = jnp.dot(
        chooser, ffn_in.reshape(routed, ROWS * width), preferred_element_type=jnp.float32
    )
    outgoing = outgoing.astype(jnp.bfloat16).reshape(owners_count, CAP, ROWS, width)
    occupied = jnp.any(hits, axis=1).astype(jnp.bfloat16).reshape(owners_count, CAP)
    arrived, live = (
        lax.all_to_all(outgoing, "seq", split_axis=0, concat_axis=0, tiled=True),
        lax.all_to_all(occupied, "seq", split_axis=0, concat_axis=0, tiled=True),
    )
    live_int = (live.reshape(slots) > 0).astype(jnp.int32)
    position = jnp.cumsum(live_int) - 1
    targets = lax.broadcasted_iota(jnp.int32, (limit, slots), 0)
    packer = ((position[None, :] == targets) & (live_int[None, :] == 1)).astype(jnp.bfloat16)
    gathered = jnp.dot(
        packer, arrived.reshape(slots, ROWS * width), preferred_element_type=jnp.float32
    )
    gathered = gathered.astype(jnp.bfloat16)
    result = expert_rows(gathered.reshape(limit * ROWS, width), w_gate[0], w_up[0], w_down[0])
    result = result.reshape(limit, ROWS * width)
    spread = jnp.dot(packer.T, result, preferred_element_type=jnp.float32)
    spread = spread.astype(jnp.bfloat16).reshape(owners_count, CAP, ROWS, width)
    answers = lax.all_to_all(spread, "seq", split_axis=0, concat_axis=0, tiled=True)
    picker = hits.T.astype(jnp.bfloat16)
    picked = jnp.dot(
        picker, answers.reshape(slots, ROWS * width), preferred_element_type=jnp.float32
    )
    picked = picked.astype(jnp.bfloat16).reshape(routed, 2, ROWS, width)
    codes = gate_codes.astype(jnp.float32)
    shares = codes / jnp.sum(codes, axis=1, keepdims=True)
    total = resid.reshape(routed, ROWS, width).astype(jnp.float32)
    total = total + shares[:, 0, None, None] * picked[:, 0].astype(jnp.float32)
    total = total + shares[:, 1, None, None] * picked[:, 1].astype(jnp.float32)
    return total.astype(jnp.bfloat16).reshape(tokens, width)


def solution(mesh):
    return jax.shard_map(
        body,
        mesh=mesh,
        in_specs=(
            P(("grp", "seq"), None),
            P(),
            P(),
            P(),
            P(),
            P(),
            P("seq", None, None),
            P("seq", None, None),
            P("seq", None, None),
            P(("grp", "seq"), None),
            P(("grp", "seq"), None),
        ),
        out_specs=P(("grp", "seq"), None),
        check_vma=False,
    )
```

profile of v0, /device:TPU:24, one launch (start us, length us, event | category | flops | bytes accessed | tf_op | source)
XLA Modules:
  0.0 1010.4 jit_solution(8345088206834349410)
XLA Ops:
  6.5 2.1 fusion.1
  8.6 8.7 fusion.27
  17.8 4.4 convert_reduce_fusion.1
  22.2 1.8 copy.77
  24.0 1.8 copy.79
  25.8 3.8 copy.58
  29.6 5.4 fusion.65
  36.2 8.2 all-to-all-start
  44.6 3.3 copy.78
  47.9 3.8 copy.73
  51.8 1.7 convert_reduce_fusion
  53.5 38.9 %all_gather.15 = f32[128,8,128]{2,1,0:T(8,128)S(1)} all-gather(f32[1,8,128]{2,1,0:T(8,128)S(1)} %bitcast.126), channel_id=1, replica_groups=mesh['grp'=4,'seq'=32] {'grp','seq'}, dimensions={0}, use_global_device_ids=true | all-gather | bytes 528384 | tf_op jit(solution)/shard_map/all_gather | solution.py:19
  92.4 4.5 fusion.66
  98.4 4.3 fusion.21
  102.7 101.1 %all-gather.3.cloned.1.call-done = f32[1024,128,128]{2,1,0:T(8,128)} async-done(((f32[8,128,128]{2,1,0:T(8,128)}), f32[1024,128,128]{2,1,0:T(8,128)}) %all-gather.3.cloned.1.call-update) | async-done | bytes 67108880 | tf_op jit(solution)/shard_map/all_gather | solution.py:19
  203.8 116.2 %while.12 = (s32[]{:T(128)}, f32[8,128,128]{2,1,0:T(8,128)S(1)}, f32[8,128]{1,0:T(8,128)S(1)}, s32[]{:T(128)}, f32[128,8,128,128]{3,2,1,0:T(8,128)}, /*index=5*/...) while((s32[]{:T(128)}, f32[8,128,128]{2,1,0:T(8,128)S(1)}, f32[8,128]{1,0:T(8,128)S(1)}, s32[]{:T(128)}, ...), condition=%wide.region_4.5_spmd, body=%wide.region_3.4_spmd.sunk | while | flops 132101 | bytes 1585295 | solution.py:27
  203.8 1.2 bitcast_add_fusion.4
  205.1 1.2 bitcast_add_fusion.4
  206.3 1.2 bitcast_add_fusion.4
  207.5 1.2 bitcast_add_fusion.4
  208.7 1.2 bitcast_add_fusion.4
  209.9 1.2 bitcast_add_fusion.4
  211.1 1.2 bitcast_add_fusion.4
  212.3 1.2 bitcast_add_fusion.4
  213.5 1.2 bitcast_add_fusion.4
  214.7 1.2 bitcast_add_fusion.4
  215.9 1.2 bitcast_add_fusion.4
  217.2 1.2 bitcast_add_fusion.4
  218.4 1.2 bitcast_add_fusion.4
  219.6 1.2 bitcast_add_fusion.4
  220.8 1.2 bitcast_add_fusion.4
  222.0 1.2 bitcast_add_fusion.4
  223.2 1.2 bitcast_add_fusion.4
  224.4 1.2 bitcast_add_fusion.4
  225.6 1.2 bitcast_add_fusion.4
  226.8 1.2 bitcast_add_fusion.4
  228.0 1.2 bitcast_add_fusion.4
  229.3 1.2 bitcast_add_fusion.4
  230.5 1.2 bitcast_add_fusion.4
  320.1 3.0 fusion.67
  323.1 9.6 multiply_reduce_fusion
  332.8 4.6 copy.62
  337.4 4.9 fusion.5
  342.3 1.2 copy-done.5
  343.5 1.7 fusion.7
  345.2 3.8 reshape.195
  349.0 18.9 %convolution_convert_fusion.1 = bf16[64,131072]{1,0:T(8,128)(2,1)} fusion(pred[64,7]{0,1:T(8,128)(4,1)S(1)} %fusion.57, bf16[7,131072]{1,0:T(8,128)(2,1)S(1)} %reshape.195), kind=kOutput, calls=%fused_computation.3 | convolution fusion | flops 125829120 | bytes 18612672 | tf_op jit(solution)/shard_map/dot_general | solution.py:115
  367.9 18.7 %copy.81 = bf16[8,8,128,1024]{3,2,1,0:T(8,128)(2,1)} copy(bf16[8,8,128,1024]{3,1,2,0:T(8,128)(2,1)} %bitcast.113) | data formatting | bytes 33554432
  386.5 42.1 %all-to-all-start.1 = ((bf16[32,2,128,1024]{3,2,1,0:T(8,128)(2,1)}), bf16[32,2,128,1024]{3,2,1,0:T(8,128)(2,1)}, u32[]{:S(2)}, u32[]{:S(2)}) async-start(bf16[32,2,128,1024]{3,2,1,0:T(8,128)(2,1)} %bitcast.110), calls=%async_computation.1 | async-start | bytes 33554432 | tf_op jit(solution)/shard_map/all_to_all | solution.py:121
  429.1 212.7 %all-to-all-done.1 = bf16[32,2,128,1024]{3,2,1,0:T(8,128)(2,1)} async-done(((bf16[32,2,128,1024]{3,2,1,0:T(8,128)(2,1)}), bf16[32,2,128,1024]{3,2,1,0:T(8,128)(2,1)}, u32[]{:S(2)}, u32[]{:S(2)}) %all-to-all-start.1) | async-done | bytes 16777248 | tf_op jit(solution)/shard_map/all_to_all | solution.py:121
  641.8 18.7 %copy.82 = bf16[8,8,128,1024]{3,1,2,0:T(8,128)(2,1)} copy(bf16[8,8,128,1024]{3,2,1,0:T(8,128)(2,1)} %bitcast.43) | data formatting | bytes 33554432
  660.5 11.3 %convolution_convert_fusion.2 = bf16[28,131072]{1,0:T(8,128)(2,1)} fusion(bf16[64,131072]{1,0:T(8,128)(2,1)} %bitcast.109, s32[64]{0:T(128)S(1)} %add_reduce_fusion, pred[64]{0:T(512)(128)(4,1)S(1)} %eq.57), kind=kOutput, calls=%fused_computation.4 | convolution fusion | flops 473435648 | bytes 24117568 | tf_op jit(solution)/shard_map/dot_general | solution.py:128
  671.8 9.3 reshape.198
  681.1 12.7 %fusion.32 = f32[3584,896]{1,0:T(8,128)} fusion(bf16[3584,1024]{1,0:T(8,128)(2,1)} %reshape.198, bf16[1,1024,896]{2,1,0:T(8,128)(2,1)S(1)} %copy-done.12), kind=kOutput, calls=%fused_computation.56 | convolution fusion | flops 6576668672 | bytes 22020096 | tf_op jit(solution)/shard_map/dot_general | solution.py:39
  693.9 21.5 %convolution_convert_fusion.4 = bf16[3584,1024]{1,0:T(8,128)(2,1)} fusion(f32[3584,896]{1,0:T(8,128)} %fusion.32, bf16[3584,1024]{1,0:T(8,128)(2,1)} %reshape.198, bf16[1,896,1024]{2,1,0:T(8,128)(2,1)} %param.21, bf16[1,1024,896]{2,1,0:T(8,128)(2,1)} %param.20), kind=kOutput, calls=%fused_computation.11 | convolution fusion | flops 13176274944 | bytes 31195136 | tf_op jit(solution)/shard_map/dot_general | solution.py:42
  715.4 8.9 reshape.199
  724.3 13.6 %convolution_convert_fusion = bf16[64,131072]{1,0:T(8,128)(2,1)} fusion(bf16[28,131072]{1,0:T(8,128)(2,1)} %reshape.199, s32[64]{0:T(128)S(1)} %add_reduce_fusion, pred[64]{0:T(512)(128)(4,1)S(1)} %eq.57), kind=kOutput, calls=%fused_computation.2 | convolution fusion | flops 478154240 | bytes 24117568 | tf_op jit(solution)/shard_map/dot_general | solution.py:134
  737.9 18.6 %copy.83 = bf16[8,8,128,1024]{3,2,1,0:T(8,128)(2,1)} copy(bf16[8,8,128,1024]{3,1,2,0:T(8,128)(2,1)} %bitcast.112) | data formatting | bytes 33554432
  756.6 5.5 all-to-all-start.2
  762.3 213.0 %all-to-all-done.2 = bf16[32,2,128,1024]{3,2,1,0:T(8,128)(2,1)} async-done(((bf16[32,2,128,1024]{3,2,1,0:T(8,128)(2,1)}), bf16[32,2,128,1024]{3,2,1,0:T(8,128)(2,1)}, u32[]{:S(2)}, u32[]{:S(2)}) %all-to-all-start.2) | async-done | bytes 16777248 | tf_op jit(solution)/shard_map/all_to_all | solution.py:136
  975.2 15.3 %copy.84 = bf16[8,8,128,1024]{3,1,2,0:T(8,128)(2,1)S(1)} copy(bf16[8,8,128,1024]{3,2,1,0:T(8,128)(2,1)} %bitcast.49) | data formatting | bytes 33554432
  990.6 3.9 convolution_convert_fusion.3
  994.4 4.5 copy.85
  1000.9 2.3 fusion.9
  (232 shorter events, 92.5 us)
Async XLA Ops:
  6.5 330.8 %copy-start = (bf16[1024,1024]{1,0:T(8,128)(2,1)S(1)}, bf16[1024,1024]{1,0:T(8,128)(2,1)}, u32[]{:S(2)}) copy-start(bf16[1024,1024]{1,0:T(8,128)(2,1)} %param.17) | copy-start | bytes 6291460
  6.5 197.2 %all-gather.3.cloned.1.call-start = ((), (), s32[]{:S(2)}) async-start(), calls=%async_computation.3 | async-start | bytes 67633152 | tf_op jit(solution)/shard_map/all_gather | solution.py:19
  29.6 5.4 copy-start.8
  35.4 9.1 copy-start.10
  36.2 350.3 %all-to-all-start = ((bf16[32,1,2]{2,1,0:T(2,128)(2,1)}), bf16[32,1,2]{2,1,0:T(2,128)(2,1)S(1)}, u32[]{:S(2)}, u32[]{:S(2)}) async-start(bf16[32,1,2]{2,1,0:T(2,128)(2,1)} %reshape.210), calls=%async_computation | async-start | bytes 32768 | tf_op jit(solution)/shard_map/all_to_all | solution.py:122
  92.4 4.5 copy-start.2
  92.4 4.5 copy-start.4
  96.9 1.5 copy-start.3
  332.8 4.6 copy-start.13
  337.4 6.1 copy-start.7
  342.3 1.2 copy-start.5
  386.5 255.3 %all-to-all-start.1 = ((bf16[32,2,128,1024]{3,2,1,0:T(8,128)(2,1)}), bf16[32,2,128,1024]{3,2,1,0:T(8,128)(2,1)}, u32[]{:S(2)}, u32[]{:S(2)}) async-start(bf16[32,2,128,1024]{3,2,1,0:T(8,128)(2,1)} %bitcast.110), calls=%async_computation.1 | async-start | bytes 33554432 | tf_op jit(solution)/shard_map/all_to_all | solution.py:121
  671.8 9.3 copy-start.12
  756.6 5.6 copy-start.9
  756.6 218.6 %all-to-all-start.2 = ((bf16[32,2,128,1024]{3,2,1,0:T(8,128)(2,1)}), bf16[32,2,128,1024]{3,2,1,0:T(8,128)(2,1)}, u32[]{:S(2)}, u32[]{:S(2)}) async-start(bf16[32,2,128,1024]{3,2,1,0:T(8,128)(2,1)} %bitcast.111), calls=%async_computation.2 | async-start | bytes 33554432 | tf_op jit(solution)/shard_map/all_to_all | solution.py:136
  975.2 15.3 %copy-start.11 = (s32[14]{0:T(128)S(1)}, s32[14]{0:T(128)}, u32[]{:S(2)}) copy-start(s32[14]{0:T(128)} %copy-done.10) | copy-start | bytes 172
  999.4 1.5 copy-start.6
  999.9 3.3 copy-start.1
Sparse Core Ops, SparseCore 0:
  35.1 168.6 all-gather.2
where the time goes:
time: 1030 us; the launch traced here: 1010 us
  waiting for transfers between devices  527 us (51%)
  other arithmetic  131 us (13%)
  local copies, waits for them, and re-layouts  122 us (12%)
  matrix products  119 us (12%)
  starting transfers between devices  55.8 us (5%)
  blocking collectives  38.9 us (4%)
  between operations  14.1 us (1%)
    all_to_all x1, waiting for transfers between devices, body(): lax.all_to_all(spread, 'seq', split_axis=0, concat_axis=0, tiled=True)  213 us
    all_to_all x1, waiting for transfers between devices, body(): lax.all_to_all(outgoing, 'seq', split_axis=0, concat_axis=0, tiled=True)  213 us
    add x192, other arithmetic, add_pair(): return (earlier[0] + later[0], earlier[1] + later[1])  113 us
    all_gather x1, waiting for transfers between devices, carried_in(): gathered = jax.tree.map(lambda a: lax.all_gather(a, axis), part)  101 us
    unnamed x39, local copies, waits for them, and re-layouts  86.6 us
    all_to_all x1, starting transfers between devices, body(): lax.all_to_all(outgoing, 'seq', split_axis=0, concat_axis=0, tiled=True)  42.1 us
    all_gather x1, blocking collectives, carried_in(): gathered = jax.tree.map(lambda a: lax.all_gather(a, axis), part)  38.9 us
    dot_general x1, matrix products, expert_rows(): jnp.dot(inner, down_weight, preferred_element_type=jnp.float32)  21.5 us
  transfers between devices with their start and end apart: 4, of which 3 were waited for; matrix products, arithmetic and copies ran while one was open for 20% of the time, Pallas kernels for 0%

commit v1 on v0

v1 whole, which is shorter than its diff:
```python
import functools

import jax
import jax.numpy as jnp
from jax import lax
from jax.experimental import pallas as pl
from jax.experimental.pallas import tpu as pltpu
from jax.sharding import PartitionSpec as P

HEADS = 8
HEAD_DIM = 128
ROWS = 128
EPS = 1e-06
WAYS = 4
CORES = 2
SLOTS = 4
CHUNKS = 8
STATE = 144
LIMIT = 14
MESH = pl.DeviceIdType.MESH
F32 = jnp.float32
BF16 = jnp.bfloat16
LIMIT_BYTES = 60 * 1024 * 1024


def place():
    seq = lax.axis_index("seq")
    return lax.axis_index("grp"), seq // (WAYS * CORES), (seq // CORES) % WAYS, seq % CORES


def remote(src, dst, send, recv, device):
    return pltpu.make_async_remote_copy(
        src_ref=src, dst_ref=dst, send_sem=send, recv_sem=recv, device_id=device, device_id_type=MESH
    )


def greet(devices):
    barrier = pltpu.get_barrier_semaphore()
    for device in devices:
        pl.semaphore_signal(barrier, inc=1, device_id=device, device_id_type=MESH)
    pl.semaphore_wait(barrier, len(devices))


def norm_rows(values, gain):
    return values * lax.rsqrt(jnp.mean(values * values, axis=-1, keepdims=True) + EPS) * gain


def dot_last(a, b):
    return lax.dot_general(a, b, (((1,), (1,)), ((), ())), preferred_element_type=F32)


def dot_first(a, b):
    return lax.dot_general(a, b, (((0,), (0,)), ((), ())), preferred_element_type=F32)


def lifted(values):
    return jnp.where(values > 0.0, values + 1.0, jnp.exp(jnp.minimum(values, 0.0))).astype(BF16)


def qkv_kernel(x_ref, gain_ref, wq_ref, wk_ref, wv_ref, q_ref, k_ref, v_ref, st_ref, normed):
    tokens = x_ref.shape[0]

    @pl.when(pl.program_id(0) == 0)
    def _():
        @pl.loop(0, tokens // ROWS)
        def _(i):
            rows = pl.ds(pl.multiple_of(i * ROWS, ROWS), ROWS)
            normed[rows, :] = norm_rows(x_ref[rows, :].astype(F32), gain_ref[...]).astype(BF16)

    q_ref[...] = lifted(jnp.dot(normed[...], wq_ref[...], preferred_element_type=F32))
    k_ref[...] = lifted(jnp.dot(normed[...], wk_ref[...], preferred_element_type=F32))
    v_ref[...] = jnp.dot(normed[...], wv_ref[...], preferred_element_type=F32).astype(BF16)
    for head in range(q_ref.shape[1] // HEAD_DIM):
        cols = slice(head * HEAD_DIM, (head + 1) * HEAD_DIM)
        keys = k_ref[:, cols]
        st_ref[head, :HEAD_DIM, :] = dot_first(v_ref[:, cols], keys)
        total = jnp.sum(keys.astype(F32), axis=0, keepdims=True)
        st_ref[head, HEAD_DIM:, :] = jnp.broadcast_to(total, (STATE - HEAD_DIM, HEAD_DIM))


def qkv(x, gain, w_qkv):
    tokens, width = x.shape
    step = 2 * HEAD_DIM
    steps = width // step
    column = pl.BlockSpec((tokens, step), lambda j: (0, j))
    return pl.pallas_call(
        qkv_kernel,
        grid=(steps,),
        out_shape=[jax.ShapeDtypeStruct((tokens, width), BF16)] * 3
        + [jax.ShapeDtypeStruct((width // HEAD_DIM, STATE, HEAD_DIM), F32)],
        in_specs=[
            pl.BlockSpec((tokens, width), lambda j: (0, 0)),
            pl.BlockSpec((1, width), lambda j: (0, 0)),
            pl.BlockSpec((width, step), lambda j: (0, j)),
            pl.BlockSpec((width, step), lambda j: (0, steps + j)),
            pl.BlockSpec((width, step), lambda j: (0, 2 * steps + j)),
        ],
        out_specs=[column] * 3 + [pl.BlockSpec((2, STATE, HEAD_DIM), lambda j: (j, 0, 0))],
        scratch_shapes=[pltpu.VMEM((tokens, width), BF16)],
        compiler_params=pltpu.CompilerParams(vmem_limit_bytes=LIMIT_BYTES),
        name="qkv",
    )(x, gain, w_qkv, w_qkv, w_qkv)


def prefix_kernel(
    groups, st_ref, out_ref, mine, sib, chips, xs, row_sum, zs, plane_sum, ys, back, heads_in, sib2,
    send, recv,
):
    y, z, x, c = place()
    lane = WAYS * CORES

    def at(yy, zz, xx, cc):
        return (yy, zz * lane + xx * CORES + cc)

    sibling = at(y, z, x, 1 - c)
    along_x = [at(y, z, (x + d) % WAYS, c) for d in range(1, WAYS)]
    along_z = [at(y, (z + d) % WAYS, x, c) for d in range(1, WAYS)]
    along_y = [at((y + d) % groups, z, x, c) for d in range(1, groups)]
    greet([sibling] + along_x + along_z + along_y)
    copies = []

    def go(src, dst, device):
        n = len(copies)
        copy = remote(src, dst, send.at[n], recv.at[n], device)
        copy.start()
        copies.append(copy)
        return copy

    mine[...] = st_ref[...].astype(BF16)
    swap = go(mine, sib, sibling)
    swap.wait_recv()
    base = c * WAYS
    for i in range(WAYS):
        chips[i] = (st_ref[base + i] + sib[base + i].astype(F32)).astype(BF16)
    xs[x] = chips[x]
    waits = [go(chips.at[(x + d) % WAYS], xs.at[x], along_x[d - 1]) for d in range(1, WAYS)]
    for copy in waits:
        copy.wait_recv()
    row_sum[...] = sum(xs[i].astype(F32) for i in range(WAYS)).astype(BF16)
    zs[z] = row_sum[...]
    waits = [go(row_sum, zs.at[z], along_z[d - 1]) for d in range(1, WAYS)]
    for copy in waits:
        copy.wait_recv()
    plane_sum[...] = sum(zs[i].astype(F32) for i in range(WAYS)).astype(BF16)
    waits = [go(plane_sum, ys.at[y], along_y[d - 1]) for d in range(1, groups)]
    total = jnp.zeros(row_sum.shape, F32)
    for i in range(WAYS):
        total = total + zs[i].astype(F32) * jnp.where(i < z, 1.0, 0.0)
    for copy in waits:
        copy.wait_recv()
    ys[y] = plane_sum[...]
    for i in range(groups):
        total = total + ys[i].astype(F32) * jnp.where(i < y, 1.0, 0.0)
    for i in range(WAYS):
        back[i] = total.astype(BF16)
        total = total + xs[i].astype(F32)
    heads_in[x] = back[x]
    waits = [go(back.at[(x + d) % WAYS], heads_in.at[x], along_x[d - 1]) for d in range(1, WAYS)]
    for copy in waits:
        copy.wait_recv()
    swap = go(heads_in, sib2, sibling)
    later = jnp.where(c == 1, 1.0, 0.0)
    for i in range(WAYS):
        mixed = heads_in[i].astype(F32) + sib[base + i].astype(F32) * later
        out_ref[base + i] = mixed.astype(BF16)
    swap.wait_recv()
    base = (1 - c) * WAYS
    for i in range(WAYS):
        mixed = sib2[i].astype(F32) + sib[base + i].astype(F32) * later
        out_ref[base + i] = mixed.astype(BF16)
    for copy in copies:
        copy.wait_send()


def prefix(state, groups):
    one = (STATE, HEAD_DIM)
    some = (WAYS,) + one
    count = 2 + 2 * (WAYS - 1) + (WAYS - 1) + groups - 1
    return pl.pallas_call(
        functools.partial(prefix_kernel, groups),
        out_shape=jax.ShapeDtypeStruct(state.shape, BF16),
        in_specs=[pl.BlockSpec(memory_space=pltpu.VMEM)],
        out_specs=pl.BlockSpec(memory_space=pltpu.VMEM),
        scratch_shapes=[
            pltpu.VMEM(state.shape, BF16),
            pltpu.VMEM(state.shape, BF16),
            pltpu.VMEM(some, BF16),
            pltpu.VMEM(some, BF16),
            pltpu.VMEM(one, BF16),
            pltpu.VMEM(some, BF16),
            pltpu.VMEM(one, BF16),
            pltpu.VMEM((groups,) + one, BF16),
            pltpu.VMEM(some, BF16),
            pltpu.VMEM(some, BF16),
            pltpu.VMEM(some, BF16),
            pltpu.SemaphoreType.DMA((count,)),
            pltpu.SemaphoreType.DMA((count,)),
        ],
        compiler_params=pltpu.CompilerParams(collective_id=0, has_side_effects=True),
        name="prefix",
    )(state)


def attend_kernel(
    x_ref, q_ref, k_ref, v_ref, prior_ref, hgain_ref, wout_ref, fgain_ref, resid_ref, ffn_ref, ratio
):
    tokens = x_ref.shape[0]
    tiles = tokens // ROWS
    causal = lax.broadcasted_iota(jnp.int32, (ROWS, ROWS), 0) >= lax.broadcasted_iota(
        jnp.int32, (ROWS, ROWS), 1
    )

    @pl.loop(0, HEADS)
    def _(head):
        cols = pl.ds(pl.multiple_of(head * HEAD_DIM, HEAD_DIM), HEAD_DIM)
        keys = k_ref[:, cols]
        wide = jnp.concatenate([v_ref[:, cols], jnp.ones((tokens, HEAD_DIM), BF16)], axis=1)
        prior = prior_ref[head]
        counts = jnp.broadcast_to(prior[HEAD_DIM : HEAD_DIM + 1, :], (HEAD_DIM, HEAD_DIM))
        carried = jnp.concatenate([prior[:HEAD_DIM, :], counts], axis=0)
        for tile in range(tiles):
            rows = slice(tile * ROWS, (tile + 1) * ROWS)
            query = q_ref[rows, cols]
            numer = dot_last(query, carried)
            scores = jnp.where(causal, dot_last(query, keys[rows, :]), 0.0).astype(BF16)
            numer = numer + jnp.dot(scores, wide[rows, :], preferred_element_type=F32)
            if tile > 0:
                scores = dot_last(query, keys[: tile * ROWS, :]).astype(BF16)
                numer = numer + jnp.dot(
                    scores, wide[: tile * ROWS, :], preferred_element_type=F32
                )
            ratio[rows, cols] = numer[:, :HEAD_DIM] / numer[:, HEAD_DIM:]

    half = tokens // 2
    for part in range(2):
        rows = slice(part * half, (part + 1) * half)
        attended = norm_rows(ratio[rows, :], hgain_ref[...]).astype(BF16)
        resid = x_ref[rows, :].astype(F32) + jnp.dot(
            attended, wout_ref[...], preferred_element_type=F32
        )
        resid = resid.astype(BF16)
        resid_ref[rows, :] = resid
        ffn_ref[rows, :] = norm_rows(resid.astype(F32), fgain_ref[...]).astype(BF16)


def attend(x, q, k, v, prior, head_gain, w_out, ffn_gain):
    tokens, width = x.shape
    return pl.pallas_call(
        attend_kernel,
        out_shape=[jax.ShapeDtypeStruct((tokens, width), BF16)] * 2,
        in_specs=[pl.BlockSpec(memory_space=pltpu.VMEM)] * 8,
        out_specs=[pl.BlockSpec(memory_space=pltpu.VMEM)] * 2,
        scratch_shapes=[pltpu.VMEM((tokens, width), F32)],
        compiler_params=pltpu.CompilerParams(vmem_limit_bytes=LIMIT_BYTES),
        name="attend",
    )(x, q, k, v, prior, head_gain, w_out, ffn_gain)


def neighbours():
    y, z, x, c = place()
    lane = WAYS * CORES

    def at(zz, xx, cc):
        return (y, ((zz + WAYS) % WAYS) * lane + ((xx + WAYS) % WAYS) * CORES + cc)

    return (
        at(z, x, 1 - c), at(z, x + 1, c), at(z, x - 1, c), at(z + 1, x, c), at(z - 1, x, c)
    )


def dispatch_kernel(blocks, table, f_ref, out_ref, *rest):
    chunks = out_ref.shape[0]
    depth = out_ref.shape[2]
    gather = rest[:chunks]
    stage, relay, local, send, recv = rest[chunks:]
    y, z, x, c = place()
    sibling, right, left, up, down = neighbours()
    greet([sibling, right, left, up, down])
    me = (x * CORES + c) * blocks
    from_left = (((x + WAYS - 1) % WAYS) * CORES + c) * blocks
    from_right = (((x + 1) % WAYS) * CORES + c) * blocks
    from_far = (((x + 2) % WAYS) * CORES + c) * blocks
    pending = []

    def go(k, n, src, dst, device):
        copy = remote(src, dst, send.at[k, n], recv.at[k, n], device)
        copy.start()
        pending.append(copy)
        return copy

    made = {}

    def begin(k):
        own = f_ref.at[:, pl.ds(k * depth, depth), :]
        here = gather[k].at[pl.ds(me, blocks)]
        made[k, 0] = go(k, 0, own, here, right)
        made[k, 1] = go(k, 1, own, here, left)
        made[k, 2] = go(k, 2, own, here, sibling)
        keep = pltpu.make_async_copy(own, here, local.at[k])
        keep.start()
        made[k, "keep"] = keep

    def spread(k):
        def pass_on(n, start):
            part = gather[k].at[pl.ds(start, blocks)]
            made[k, n] = go(k, n, part, part, sibling)

        first, second = (0, 1) if k % 2 == 0 else (1, 0)
        nearer, farther = (from_left, from_right) if k % 2 == 0 else (from_right, from_left)
        made[k, first].wait_recv()
        part = gather[k].at[pl.ds(nearer, blocks)]
        made[k, 3] = go(k, 3, part, part, right if k % 2 == 0 else left)
        if k + 2 < chunks:
            begin(k + 2)
        pass_on(4, nearer) if k % 2 == 0 else pass_on(5, nearer)
        made[k, second].wait_recv()
        pass_on(5, farther) if k % 2 == 0 else pass_on(4, farther)
        made[k, 3].wait_recv()
        pass_on(6, from_far)

    def select(k):
        made[k, "keep"].wait()
        for n in (2, 4, 5, 6):
            made[k, n].wait_recv()
        for d in (2, 1, 3, 0):
            target = (z + d) % WAYS
            for j in range(SLOTS):
                rows = gather[k][table[target * SLOTS + j]]
                if d == 0:
                    out_ref[k, z * SLOTS + j] = rows
                else:
                    stage[k, d - 1, j] = rows
            if d == 2:
                made[k, 7] = go(k, 7, stage.at[k, 1], relay.at[k], up if k % 2 == 0 else down)
            if d == 1:
                made[k, 8] = go(k, 8, stage.at[k, 0], out_ref.at[k, pl.ds(z * SLOTS, SLOTS)], up)
            if d == 3:
                made[k, 9] = go(k, 9, stage.at[k, 2], out_ref.at[k, pl.ds(z * SLOTS, SLOTS)], down)

    def forward(k):
        made[k, 7].wait_recv()
        origin = (z + WAYS - 1) % WAYS if k % 2 == 0 else (z + 1) % WAYS
        made[k, 10] = go(
            k, 10, relay.at[k], out_ref.at[k, pl.ds(origin * SLOTS, SLOTS)],
            up if k % 2 == 0 else down,
        )

    begin(0)
    if chunks > 1:
        begin(1)
    for step in range(chunks + 2):
        if step < chunks:
            spread(step)
        if 1 <= step <= chunks:
            select(step - 1)
        if step >= 2:
            forward(step - 2)
    for k in range(chunks):
        for n in (8, 9, 10):
            made[k, n].wait_recv()
    for copy in pending:
        copy.wait_send()


def dispatch(table, ffn_in):
    blocks, rows, width = ffn_in.shape
    chunks = CHUNKS
    depth = rows // chunks
    slots = WAYS * SLOTS
    row = WAYS * CORES * blocks
    return pl.pallas_call(
        functools.partial(dispatch_kernel, blocks),
        out_shape=jax.ShapeDtypeStruct((chunks, slots, depth, width), BF16),
        in_specs=[
            pl.BlockSpec(memory_space=pltpu.SMEM),
            pl.BlockSpec(memory_space=pltpu.VMEM),
        ],
        out_specs=pl.BlockSpec(memory_space=pltpu.VMEM),
        scratch_shapes=[pltpu.VMEM((row, depth, width), BF16)] * chunks
        + [
            pltpu.VMEM((chunks, WAYS - 1, SLOTS, depth, width), BF16),
            pltpu.VMEM((chunks, SLOTS, depth, width), BF16),
            pltpu.SemaphoreType.DMA((chunks,)),
            pltpu.SemaphoreType.DMA((chunks, 11)),
            pltpu.SemaphoreType.DMA((chunks, 11)),
        ],
        compiler_params=pltpu.CompilerParams(
            collective_id=1, has_side_effects=True, vmem_limit_bytes=LIMIT_BYTES
        ),
        name="dispatch",
    )(table, ffn_in)


def combine_kernel(
    blocks, index, weight, hot_index, hot_weight, res_ref, resid_ref, hot_ref, out_ref, *rest
):
    chunks, slots, depth, width = res_ref.shape
    results = rest[:chunks]
    partial, relay, merge, final, local, send, recv = rest[chunks:]
    y, z, x, c = place()
    sibling, right, left, up, down = neighbours()
    greet([sibling, right, left, up, down])
    pending = []
    made = {}

    def go(k, n, src, dst, device):
        copy = remote(src, dst, send.at[k, n], recv.at[k, n], device)
        copy.start()
        pending.append(copy)
        made[k, n] = copy

    def slot(row):
        return pl.ds(c * slots + row * SLOTS, SLOTS)

    def part(row):
        return pl.ds(((row + WAYS) % WAYS) * SLOTS, SLOTS)

    def begin(k):
        far = up if k % 2 == 0 else down
        go(k, 2, res_ref.at[k, part(z + 2)], relay.at[k], far)
        go(k, 0, res_ref.at[k, part(z + 1)], results[k].at[slot(z)], up)
        go(k, 1, res_ref.at[k, part(z - 1)], results[k].at[slot(z)], down)
        keep = pltpu.make_async_copy(res_ref.at[k, part(z)], results[k].at[slot(z)], local.at[k])
        keep.start()
        made[k, "keep"] = keep

    def share(k):
        made[k, 2].wait_recv()
        origin = (z + WAYS - 1) % WAYS if k % 2 == 0 else (z + 1) % WAYS
        go(k, 3, relay.at[k], results[k].at[slot(origin)], up if k % 2 == 0 else down)
        if k + 2 < chunks:
            begin(k + 2)
        made[k, "keep"].wait()
        for n in (0, 1, 3):
            made[k, n].wait_recv()
        here = results[k].at[pl.ds(c * slots, slots)]
        go(k, 4, here, here, sibling)

    def build(k):
        made[k, 4].wait_recv()

        def one(n, carry):
            first = results[k][index[2 * n]].astype(F32) * weight[2 * n]
            second = results[k][index[2 * n + 1]].astype(F32) * weight[2 * n + 1]
            partial[k, n] = (first + second).astype(BF16)
            return carry

        def ways(d):
            return partial.at[k, pl.ds(d * blocks, blocks)]

        lax.fori_loop(2 * blocks, 3 * blocks, one, 0)
        go(k, 5, ways(2), merge.at[k], right if k % 2 == 0 else left)
        if k % 2 == 0:
            lax.fori_loop(3 * blocks, 4 * blocks, one, 0)
            go(k, 7, ways(3), final.at[k, 1], left)
            lax.fori_loop(0, 2 * blocks, one, 0)
        else:
            lax.fori_loop(blocks, 2 * blocks, one, 0)
            go(k, 6, ways(1), final.at[k, 0], right)
            lax.fori_loop(3 * blocks, 4 * blocks, one, 0)
            lax.fori_loop(0, blocks, one, 0)

    def join(k):
        made[k, 5].wait_recv()
        d = 1 if k % 2 == 0 else 3

        def one(b, carry):
            there = d * blocks + b
            partial[k, there] = (
                partial[k, there].astype(F32) + merge[k, b].astype(F32)
            ).astype(BF16)
            return carry

        lax.fori_loop(0, blocks, one, 0)
        ready = partial.at[k, pl.ds(d * blocks, blocks)]
        if k % 2 == 0:
            go(k, 6, ready, final.at[k, 0], right)
        else:
            go(k, 7, ready, final.at[k, 1], left)

    def finish(k):
        made[k, 6].wait_recv()
        made[k, 7].wait_recv()
        rows = slice(k * depth, (k + 1) * depth)

        def one(b, carry):
            total = resid_ref[b, rows, :].astype(F32) + partial[k, b].astype(F32)
            total = total + final[k, 0, b].astype(F32) + final[k, 1, b].astype(F32)
            total = total + hot_ref[hot_index[b]][rows, :].astype(F32) * hot_weight[b]
            out_ref[b, rows, :] = total.astype(BF16)
            return carry

        lax.fori_loop(0, blocks, one, 0)

    begin(0)
    if chunks > 1:
        begin(1)
    for step in range(chunks + 3):
        if step < chunks:
            share(step)
        if 1 <= step <= chunks:
            build(step - 1)
        if 2 <= step <= chunks + 1:
            join(step - 2)
        if step >= 3:
            finish(step - 3)
    for copy in pending:
        copy.wait_send()


def combine(tables, results, resid, hot_out):
    chunks, slots, depth, width = results.shape
    blocks = resid.shape[0]
    return pl.pallas_call(
        functools.partial(combine_kernel, blocks),
        out_shape=jax.ShapeDtypeStruct(resid.shape, BF16),
        in_specs=[pl.BlockSpec(memory_space=pltpu.SMEM)] * 4
        + [pl.BlockSpec(memory_space=pltpu.VMEM)] * 3,
        out_specs=pl.BlockSpec(memory_space=pltpu.VMEM),
        scratch_shapes=[pltpu.VMEM((CORES * slots, depth, width), BF16)] * chunks
        + [
            pltpu.VMEM((chunks, WAYS * blocks, depth, width), BF16),
            pltpu.VMEM((chunks, SLOTS, depth, width), BF16),
            pltpu.VMEM((chunks, blocks, depth, width), BF16),
            pltpu.VMEM((chunks, 2, blocks, depth, width), BF16),
            pltpu.SemaphoreType.DMA((chunks,)),
            pltpu.SemaphoreType.DMA((chunks, 8)),
            pltpu.SemaphoreType.DMA((chunks, 8)),
        ],
        compiler_params=pltpu.CompilerParams(
            collective_id=2, has_side_effects=True, vmem_limit_bytes=LIMIT_BYTES
        ),
        name="combine",
    )(*tables, results, resid, hot_out)


def expert_kernel(x_ref, gate_ref, up_ref, down_ref, out_ref):
    rows = x_ref[...]
    gate = jnp.dot(rows, gate_ref[...], preferred_element_type=F32)
    upper = jnp.dot(rows, up_ref[...], preferred_element_type=F32)
    inner = (jax.nn.silu(gate) * upper).astype(BF16)
    out_ref[...] = jnp.dot(inner, down_ref[...], preferred_element_type=F32).astype(BF16)


def experts(rows, w_gate, w_up, w_down, step):
    count, width = rows.shape
    hidden = w_gate.shape[1]
    once = pl.Buffered(1)
    return pl.pallas_call(
        expert_kernel,
        grid=(count // step,),
        out_shape=jax.ShapeDtypeStruct((count, width), BF16),
        in_specs=[
            pl.BlockSpec((step, width), lambda i: (i, 0)),
            pl.BlockSpec((width, hidden), lambda i: (0, 0), pipeline_mode=once),
            pl.BlockSpec((width, hidden), lambda i: (0, 0), pipeline_mode=once),
            pl.BlockSpec((hidden, width), lambda i: (0, 0), pipeline_mode=once),
        ],
        out_specs=pl.BlockSpec((step, width), lambda i: (i, 0)),
        compiler_params=pltpu.CompilerParams(vmem_limit_bytes=LIMIT_BYTES),
        name="experts",
    )(rows, w_gate, w_up, w_down)


def hot_kernel(pick, x_ref, gate_ref, up_ref, down_ref, out_ref):
    expert_kernel(x_ref.at[0], gate_ref, up_ref, down_ref, out_ref.at[0])


def hot_experts(pick, ffn_in, w_gate, w_up, w_down):
    blocks, rows, width = ffn_in.shape
    hidden = w_gate.shape[1]
    return pl.pallas_call(
        hot_kernel,
        grid_spec=pltpu.PrefetchScalarGridSpec(
            num_scalar_prefetch=1,
            grid=(2,),
            in_specs=[
                pl.BlockSpec((1, rows, width), lambda i, pick: (pick[i], 0, 0)),
                pl.BlockSpec((width, hidden), lambda i, pick: (0, 0)),
                pl.BlockSpec((width, hidden), lambda i, pick: (0, 0)),
                pl.BlockSpec((hidden, width), lambda i, pick: (0, 0)),
            ],
            out_specs=pl.BlockSpec((1, rows, width), lambda i, pick: (i, 0, 0)),
        ),
        out_shape=jax.ShapeDtypeStruct((2, rows, width), BF16),
        compiler_params=pltpu.CompilerParams(vmem_limit_bytes=LIMIT_BYTES),
        name="hot_experts",
    )(pick, ffn_in, w_gate, w_up, w_down)


def routing(pair_ids, gate_codes):
    y, z, x, c = place()
    blocks = pair_ids.shape[0]
    row = WAYS * CORES * blocks * 2
    mine = jnp.concatenate([pair_ids, gate_codes], axis=1)
    everyone = lax.all_gather(mine, ("grp", "seq"))
    ids = everyone[:, :, :2].reshape(-1, row)
    groups = ids.shape[0] // WAYS
    owners = lax.axis_size("seq")
    before = lax.broadcasted_iota(jnp.int32, (row, row), 1) < lax.broadcasted_iota(
        jnp.int32, (row, row), 0
    )
    same = ids[:, :, None] == ids[:, None, :]
    rank = jnp.sum((same & before[None]).astype(jnp.int32), axis=2)
    numbers = jnp.arange(owners, dtype=jnp.int32)
    counts = jnp.sum(
        (ids.reshape(groups, -1)[:, :, None] == numbers[None, None, :]).astype(jnp.int32), axis=1
    )
    hot = jnp.argmax(counts, axis=1).astype(jnp.int32)
    cold = ids != jnp.repeat(hot, WAYS)[:, None]
    rounds = jnp.max(jnp.where(cold, rank, 0)) // SLOTS + 1
    my_hot = hot[y]
    my_ids = ids[y * WAYS + z]
    my_rank = rank[y * WAYS + z]
    codes = everyone[:, :, 2:].reshape(-1, row)[y * WAYS + z].reshape(-1, 2).astype(F32)
    shares = codes / jnp.sum(codes, axis=1, keepdims=True)
    own_hot = pair_ids == my_hot
    own_codes = gate_codes.astype(F32)
    own_shares = own_codes / jnp.sum(own_codes, axis=1, keepdims=True)
    hot_weight = jnp.sum(jnp.where(own_hot, own_shares, 0.0), axis=1)
    any_hot = jnp.any(own_hot, axis=1).astype(jnp.int32)
    hot_index = jnp.clip(jnp.cumsum(any_hot) - any_hot, 0, 1)
    numbers = jnp.arange(blocks, dtype=jnp.int32)
    pick = jnp.stack(
        [jnp.sum(numbers * any_hot * (hot_index == i).astype(jnp.int32)) for i in range(2)]
    )
    return my_ids, my_rank, shares, my_hot, rounds, hot_weight, hot_index, pick


def round_tables(info, turn, blocks):
    y, z, x, c = place()
    my_ids, my_rank, shares, my_hot = info
    visits = my_ids.shape[0]
    place_of = my_rank - turn * SLOTS
    usable = (my_ids != my_hot) & (place_of >= 0) & (place_of < SLOTS)
    slots = jnp.arange(WAYS * SLOTS, dtype=jnp.int32)
    expert = (slots // SLOTS) * (WAYS * CORES) + x * CORES + c
    hit = (
        (my_ids[None, :] == expert[:, None])
        & (place_of[None, :] == (slots % SLOTS)[:, None])
        & usable[None, :]
    )
    block = jnp.arange(visits, dtype=jnp.int32) // 2
    source = jnp.sum(jnp.where(hit, block[None, :], 0), axis=1)
    here = usable & ((my_ids // CORES) % WAYS == x)
    index = (my_ids % CORES) * (WAYS * SLOTS) + (my_ids // (WAYS * CORES)) * SLOTS + place_of
    index = jnp.where(here, index, 0)
    weight = jnp.where(here, shares.reshape(-1), 0.0)
    order = (x + jnp.arange(WAYS, dtype=jnp.int32)) % WAYS

    def mine(values):
        values = values.reshape(WAYS, CORES, blocks * 2)
        values = lax.dynamic_index_in_dim(values, c, 1, False)
        return jnp.take(values, order, axis=0).reshape(-1)

    return source, mine(index), mine(weight)


def body(
    hidden_in, attn_gain, w_qkv, head_gain, w_out, ffn_gain, w_gate, w_up, w_down, pair_ids, gate_codes
):
    tokens, width = hidden_in.shape
    blocks = tokens // ROWS
    groups = lax.axis_size("grp")
    my_ids, my_rank, shares, my_hot, rounds, hot_weight, hot_index, pick = routing(
        pair_ids, gate_codes
    )
    info = (my_ids, my_rank, shares, my_hot)
    is_mine = lax.axis_index("seq") == my_hot
    hot_weights = [
        lax.psum(jnp.where(is_mine, w[0], jnp.zeros_like(w[0])), "seq") for w in (w_gate, w_up, w_down)
    ]
    q, k, v, state = qkv(hidden_in, attn_gain[None], w_qkv)
    prior = prefix(state, groups)
    resid, ffn_in = attend(
        hidden_in, q, k, v, prior, head_gain[None], w_out, ffn_gain[None]
    )
    resid = resid.reshape(blocks, ROWS, width)
    ffn_in = ffn_in.reshape(blocks, ROWS, width)

    def turn_of(turn, base, hot_out, hot_weight):
        source, index, weight = round_tables(info, turn, blocks)
        arrived = dispatch(source, ffn_in)
        shape = arrived.shape
        result = experts(arrived.reshape(-1, width), w_gate[0], w_up[0], w_down[0], 512)
        return combine((index, weight, hot_index, hot_weight), result.reshape(shape), base, hot_out)

    hot_out = hot_experts(pick, ffn_in, *hot_weights)
    total = turn_of(0, resid, hot_out, hot_weight)

    def more(total):
        none = jnp.zeros_like(hot_weight)
        return lax.fori_loop(
            1, -(-LIMIT // SLOTS), lambda turn, t: turn_of(turn, t, hot_out, none), total
        )

    total = lax.cond(rounds > 1, more, lambda total: total, total)
    return total.reshape(tokens, width)


def solution(mesh):
    return jax.shard_map(
        body,
        mesh=mesh,
        in_specs=(
            P(("grp", "seq"), None), P(), P(), P(), P(), P(),
            P("seq", None, None), P("seq", None, None), P("seq", None, None),
            P(("grp", "seq"), None), P(("grp", "seq"), None),
        ),
        out_specs=P(("grp", "seq"), None),
        check_vma=False,
    )
```

time: 1030 us -> 354 us (0.34); the launches traced: 1010 us -> 351 us
  waiting for transfers between devices: 527 us -> 0.02 us
  Pallas kernels: 0 us -> 272 us
  matrix products: 119 us -> 0 us
  other arithmetic: 131 us -> 16.3 us
  local copies, waits for them, and re-layouts: 122 us -> 9.24 us
  starting transfers between devices: 55.8 us -> 0.01 us
    all_to_all x3 -> x0, waiting for transfers between devices: 426 us -> none  [the longest x1 213 us: body(): lax.all_to_all(spread, 'seq', split_axis=0, concat_axis=0, tiled=True)]
    pallas_call x0 -> x7, Pallas kernels: none -> 272 us  [the longest x1 101 us: dispatch(): pl.pallas_call(functools.partial(dispatch_kernel, blocks), out_shape=jax....]
    dot_general x13 -> x0, matrix products: 119 us -> none  [the longest x1 21.5 us: expert_rows(): jnp.dot(inner, down_weight, preferred_element_type=jnp.float32)]
    add x195 -> x0, other arithmetic: 113 us -> none  [the longest x192 113 us: add_pair(): return (earlier[0] + later[0], earlier[1] + later[1])]
    all_gather x1 -> x0, waiting for transfers between devices: 101 us -> none  [carried_in(): gathered = jax.tree.map(lambda a: lax.all_gather(a, axis), part)]
    unnamed x39 -> x15, local copies, waits for them, and re-layouts: 86.6 us -> 2.6 us
    all_to_all x3 -> x0, starting transfers between devices: 55.8 us -> none  [the longest x1 42.1 us: body(): lax.all_to_all(outgoing, 'seq', split_axis=0, concat_axis=0, tiled=True)]
    reshape x6 -> x3, local copies, waits for them, and re-layouts: 29.7 us -> 1.5 us  [the longest x2 1.26 us: mine(): return jnp.take(values, order, axis=0).reshape(-1)]
  transfers between devices with their start and end apart: 4 -> 1, of which waited for: 3 -> 0; matrix products, arithmetic and copies ran while one was open for 20% -> 4% of each run, Pallas kernels for 0% -> 50%
where the time goes in v1:
time: 354 us; the launch traced here: 351 us
  Pallas kernels  272 us (77%)
  blocking collectives  36.8 us (10%)
  between operations  17 us (5%)
  other arithmetic  16.3 us (5%)
  local copies, waits for them, and re-layouts  9.24 us (3%)
    pallas_call x1, Pallas kernels, dispatch(): pl.pallas_call(functools.partial(dispatch_kernel, blocks), out_shape=jax....  101 us
    pallas_call x1, Pallas kernels, combine(): pl.pallas_call(functools.partial(combine_kernel, blocks), out_shape=jax.S...  90.3 us
    all_gather x1, blocking collectives, routing(): everyone = lax.all_gather(mine, ('grp', 'seq'))  36.8 us
    pallas_call x1, Pallas kernels, prefix(): pl.pallas_call(functools.partial(prefix_kernel, groups), out_shape=jax.Sh...  24.1 us
    pallas_call x1, Pallas kernels, attend(): pl.pallas_call(attend_kernel, out_shape=[jax.ShapeDtypeStruct((tokens, wi...  19.7 us
    pallas_call x1, Pallas kernels, experts(): pl.pallas_call(expert_kernel, grid=(count // step,), out_shape=jax.ShapeD...  17.3 us
    pallas_call x1, Pallas kernels, qkv(): pl.pallas_call(qkv_kernel, grid=(steps,), out_shape=[jax.ShapeDtypeStruct...  12.7 us
  transfers between devices with their start and end apart: 1, of which 0 were waited for; matrix products, arithmetic and copies ran while one was open for 4% of the time, Pallas kernels for 50%

profile of v1, /device:TPU:24, one launch (start us, length us, event | category | flops | bytes accessed | tf_op | source)
XLA Modules:
  0.0 350.9 jit_solution(7826683239001170479)
XLA Ops:
  6.5 0.0 all-reduce.3.cloned.1.call-start
  6.5 0.7 add_bitcast_fusion
  7.2 36.8 %all-gather.1 = s32[128,7,4]{1,2,0:T(4,128)S(1)} all-gather(s32[1,7,4]{1,2,0:T(4,128)S(1)} %add_bitcast_fusion), channel_id=2, replica_groups=mesh['grp'=4,'seq'=32] {'grp','seq'}, dimensions={0}, use_global_device_ids=true | all-gather | bytes 14448 | tf_op jit(solution)/shard_map/all_gather | solution.py:596
  44.1 0.1 fusion.33
  44.2 0.9 copy.30
  45.1 0.3 eq.259
  45.3 0.2 convert_reduce_fusion.1
  45.5 0.6 iota_reduce_fusion
  46.1 0.7 dynamic_slice.47
  47.5 0.0 copy-start.1
  47.5 0.0 copy-start.4
  47.5 3.0 broadcast_select_fusion.2
  50.5 0.0 copy-done.1
  50.5 0.0 copy-done.4
  50.6 2.1 broadcast_select_fusion.3
  52.6 0.0 copy-start.6
  52.6 0.0 all-reduce.3.cloned.1.call-update
  52.7 0.2 eq.263
  52.9 0.4 copy-done.6
  53.3 0.7 fusion.31
  54.0 0.9 copy.27
  54.9 0.2 reshape.264
  55.2 0.6 convert_reduce_fusion
  55.8 0.4 reduce_sum.85
  56.3 0.1 convert_element_type.49
  56.4 0.1 reduce_sum.86
  56.5 0.1 div.138
  56.6 0.1 copy.28
  56.7 0.1 broadcast_in_dim.123
  56.8 0.1 ne.548
  56.8 0.1 ne.549
  56.9 0.1 ne.550
  57.1 0.8 select_reduce_fusion.1
  57.9 0.7 and_bitcast_fusion
  61.3 0.1 convert_element_type.48
  61.4 0.1 copy.31
  61.5 0.1 squeeze.66
  61.6 0.2 reduce-window.9
  61.7 0.5 broadcast.974
  62.3 0.7 reduce.33
  62.9 0.1 squeeze.64
  63.1 0.7 compare_and_fusion.3
  63.8 0.6 gather_fusion.3
  64.4 0.1 broadcast_select_fusion.5
  64.5 0.7 reshape.265.weight
  65.1 0.6 gather_fusion.2
  65.7 0.1 broadcast_select_fusion.6
  65.8 0.6 reshape.263.index
  66.4 12.7 %qkv.1 = (bf16[896,1024]{1,0:T(8,128)(2,1)}, bf16[896,1024]{1,0:T(8,128)(2,1)}, bf16[896,1024]{1,0:T(8,128)(2,1)}, f32[8,144,128]{2,1,0:T(8,128)}) custom-call(bf16[896,1024]{1,0:T(8,128)(2,1)} %x_ref.3, f32[1,1024]{1,0:T(1,128)} %bitcast.103, bf16[1024,3072]{1,0:T(8,128)(2,1)} %wv_ref.1, bf16[1024,3072]{1,0:T(8,128)(2,1)} %wv_ref.1, bf16[1024,3072]{1,0:T(8,128)(2,1)} %wv_ref.1), custom_call_target="tpu_custom_call" | custom-call | tf_op jit(solution)/shard_map/qkv/pallas_call | solution.py:86
  79.1 24.1 %prefix.1.prior_ref = bf16[8,144,128]{2,1,0:T(8,128)(2,1)} custom-call(f32[8,144,128]{2,1,0:T(8,128)} %get-tuple-element.539.st_ref), custom_call_target="tpu_custom_call" | custom-call | tf_op jit(solution)/shard_map/prefix/pallas_call | solution.py:179
  103.1 19.7 %attend.1 = (bf16[896,1024]{1,0:T(8,128)(2,1)}, bf16[896,1024]{1,0:T(8,128)(2,1)S(1)}) custom-call(bf16[896,1024]{1,0:T(8,128)(2,1)} %x_ref.3, bf16[896,1024]{1,0:T(8,128)(2,1)} %get-tuple-element.536.q_ref, bf16[896,1024]{1,0:T(8,128)(2,1)} %get-tuple-element.537.k_ref, bf16[896,1024]{1,0:T(8,128)(2,1)} %get-tuple-element.538.v_ref, ...), custom_call_target="tpu_custom_call" | custom-call | tf_op jit(solution)/shard_map/attend/pallas_call | solution.py:248
  122.8 0.9 select_reduce_fusion.2.table
  123.8 101.4 %dispatch.12 = bf16[8,16,16,1024]{3,2,1,0:T(8,128)(2,1)} custom-call(s32[16]{0:T(128)} %select_reduce_fusion.2.table, bf16[7,128,1024]{2,1,0:T(8,128)(2,1)S(1)} %bitcast.76), custom_call_target="tpu_custom_call" | custom-call | tf_op jit(solution)/shard_map/dispatch/pallas_call | solution.py:371
  225.2 0.0 copy-done.2
  225.2 0.0 copy-start.7
  225.2 17.3 %experts.12 = bf16[2048,1024]{1,0:T(8,128)(2,1)} custom-call(bf16[2048,1024]{1,0:T(8,128)(2,1)} %bitcast.86, bf16[1024,896]{1,0:T(8,128)(2,1)S(1)} %bitcast.79, bf16[1024,896]{1,0:T(8,128)(2,1)} %bitcast.81, bf16[896,1024]{1,0:T(8,128)(2,1)} %bitcast.83), custom_call_target="tpu_custom_call" | custom-call | tf_op jit(solution)/shard_map/experts/pallas_call | solution.py:549
  242.6 0.7 fusion.22
  243.3 1.9 pad_add_fusion.pick
  245.2 0.0 copy-done.7
  245.2 1.2 fusion.18.hot_weight
  246.4 0.0 copy-done
  246.4 6.1 %hot_experts.1.hot_ref = bf16[2,128,1024]{2,1,0:T(8,128)(2,1)} custom-call(s32[2]{0:T(128)} %pad_add_fusion.pick, bf16[7,128,1024]{2,1,0:T(8,128)(2,1)S(1)} %bitcast.77, bf16[1024,896]{1,0:T(8,128)(2,1)} %get-tuple-element.575.gate_ref, bf16[1024,896]{1,0:T(8,128)(2,1)} %get-tuple-element.576.up_ref, bf16[896,1024]{1,0:T(8,128)(2,1)} %get-tuple-element.577.down_ref), custom_call_target="tpu_custom_call" | custom-call | tf_op jit(solution)/shard_map/hot_experts/pallas_call | solution.py:572
  252.5 90.3 %combine.12 = bf16[7,128,1024]{2,1,0:T(8,128)(2,1)S(1)} custom-call(s32[56]{0:T(128)} %reshape.263.index, f32[56]{0:T(128)} %reshape.265.weight, s32[7]{0:T(128)S(1)} %get-tuple-element.878.hot_index, f32[7]{0:T(128)} %fusion.18.hot_weight, bf16[8,16,16,1024]{3,2,1,0:T(8,128)(2,1)} %bitcast.85, bf16[7,128,1024]{2,1,0:T(8,128)(2,1)} %bitcast.89, ...), custom_call_target="tpu_custom_call" | custom-call | tf_op jit(solution)/shard_map/combine/pallas_call | solution.py:514
  342.8 1.2 copy.45
  (21 shorter events, 0.2 us)
Async XLA Ops:
  6.5 239.9 %all-reduce.3.cloned.1.call-start = ((), (), s32[]{:S(2)}) async-start(), calls=%async_computation | async-start | bytes 11010048 | tf_op jit(solution)/shard_map/psum | solution.py:671
  47.5 3.1 copy-start.1
  47.5 3.1 copy-start.4
  52.6 0.7 copy-start.6
  122.8 123.6 %copy-start = (bf16[896,1024]{1,0:T(8,128)(2,1)}, bf16[896,1024]{1,0:T(8,128)(2,1)S(1)}, u32[]{:S(2)}) copy-start(bf16[896,1024]{1,0:T(8,128)(2,1)S(1)} %get-tuple-element.540) | copy-start | bytes 5505028
  123.8 101.4 %copy-start.2 = (bf16[1,1024,896]{2,1,0:T(8,128)(2,1)S(1)}, bf16[1,1024,896]{2,1,0:T(8,128)(2,1)}, u32[]{:S(2)}) copy-start(bf16[1,1024,896]{2,1,0:T(8,128)(2,1)} %param.25) | copy-start | bytes 5505028
  225.2 20.0 %copy-start.7 = (s32[7,2]{0,1:T(2,128)S(1)}, s32[7,2]{0,1:T(2,128)}, u32[]{:S(2)}) copy-start(s32[7,2]{0,1:T(2,128)} %param.29) | copy-start | bytes 172
Sparse Core Ops, SparseCore 0:
  52.8 130.9 all-reduce.2
